TPU v7x, 32 devices: a whole 2x2x4 slice. The times are simulated.
32 devices in a mesh: energy: 16 (over z, y, x), slab: 2 (over core).
Axes of the slice: x: 2, y: 2, z: 4, core: 2. Of those that a mesh axis runs over, the one named last changes fastest.
Arguments:
- green_free: bfloat16 [16, 2, 2, 256, 256], P('energy', 'slab')
- coupling: bfloat16 [2, 2, 256, 256], P('slab'), may hold values from -0.25 to 0.25
- screened: bfloat16 [8, 2, 2, 256, 256], P(None, 'slab'), may hold values from -6 to 6
- shift_offsets: int32 [8], replicated, may hold values from -1 to 1, as said below
Outputs:
- green: bfloat16 [16, 2, 2, 256, 256], P('energy', 'slab')
- sigma: float32 [16, 2, 2, 256, 256], P('energy', 'slab')
Inputs may be any that keep to these rules, and one draw needn't show every extreme that they name: `shift_offsets`: offsets lie within one device's energy points on either side; both ends, -1 and 1, occur in every draw.
All inputs are finite; a program needn't handle non-finite values.
Results may differ from a plain program's by a relative error of at most 0.0061.
Values may be sent and summed in bfloat16 or wider, within the bound.
No kernel may reach another device: no remote copies, remote signals or barrier semaphores. Data moves between devices by JAX's collectives and lax.ppermute only.
A program may use at most 64 MiB of HBM per device.

v0:
```python
import jax
import jax.numpy as jnp
from jax import lax
from jax.sharding import PartitionSpec as P


def prefix(x, axis, combine, identity):
    size, position = (lax.axis_size(axis), lax.axis_index(axis))
    everything = jax.tree.map(
        lambda part, kind: lax.all_gather(part.astype(kind), axis),
        x,
        jax.tree.map(lambda a: jnp.bfloat16 if a.dtype == jnp.float32 else a.dtype, x),
    )
    start = jax.tree.map(
        lambda part, zero: jnp.broadcast_to(jnp.asarray(zero, part.dtype), part.shape), x, identity
    )

    def lap(k, before):
        reached = k < position
        new = combine(
            before, jax.tree.map(lambda part, own: part[k].astype(own.dtype), everything, x)
        )
        return jax.tree.map(lambda a, b: jnp.where(reached, a, b), new, before)

    return lax.fori_loop(0, size, lap, start)


def with_halo(block, sides, width):
    for axis, dim in sides:
        count = lax.axis_size(axis)
        forward = [(i, i + 1) for i in range(count - 1)]
        forward.append((count - 1, 0))
        backward = [(target, source) for source, target in forward]
        low = lax.ppermute(
            lax.slice_in_dim(block, block.shape[dim] - width, None, axis=dim), axis, forward
        )
        high = lax.ppermute(lax.slice_in_dim(block, 0, width, axis=dim), axis, backward)
        block = jnp.concatenate([low, block, high], axis=dim)
    return block


def complex_product(first, second, form):
    first_re = first[..., 0, :, :]
    first_im = first[..., 1, :, :]
    second_re = second[..., 0, :, :]
    second_im = second[..., 1, :, :]
    real = jnp.einsum(form, first_re, second_re, preferred_element_type=jnp.float32) - jnp.einsum(
        form, first_im, second_im, preferred_element_type=jnp.float32
    )
    imag = jnp.einsum(form, first_re, second_im, preferred_element_type=jnp.float32) + jnp.einsum(
        form, first_im, second_re, preferred_element_type=jnp.float32
    )
    return jnp.stack([real, imag], axis=-3)


def adjoint(block):
    real = jnp.swapaxes(block[..., 0, :, :], -1, -2)
    imag = -jnp.swapaxes(block[..., 1, :, :], -1, -2)
    return jnp.stack([real, imag], axis=-3)


def compose(earlier, later):
    early_u, early_w, early_d = earlier
    late_u, late_w, late_d = later
    joined_u = complex_product(late_u, early_u, "eij,ejk->eik").astype(jnp.bfloat16)
    joined_w = complex_product(early_w, late_w, "eij,ejk->eik").astype(jnp.bfloat16)
    partial_value = complex_product(late_u, early_d, "eij,ejk->eik").astype(jnp.bfloat16)
    joined_d = (
        late_d.astype(jnp.float32) + complex_product(partial_value, late_w, "eij,ejk->eik")
    ).astype(jnp.bfloat16)
    return (joined_u, joined_w, joined_d)


def shards(green_free, coupling, screened, shift_offsets):
    energies = green_free.shape[0]
    slabs = green_free.shape[1]
    orbitals = green_free.shape[3]
    left_map = complex_product(green_free, coupling, "esij,sjk->esik").astype(jnp.bfloat16)
    right_map = complex_product(adjoint(coupling), green_free, "sij,esjk->esik").astype(
        jnp.bfloat16
    )
    boundary = jnp.zeros((energies, 2, orbitals, orbitals), jnp.bfloat16)
    state = (left_map[:, 0], right_map[:, 0], green_free[:, 0])
    identity = jnp.eye(orbitals, dtype=jnp.float32)
    unit = jnp.stack([identity, jnp.zeros_like(identity)], axis=0)
    unit = jnp.broadcast_to(unit, (energies, 2, orbitals, orbitals)).astype(jnp.bfloat16)
    earlier = prefix(state, "slab", compose, (unit, unit, boundary))
    current = earlier[2]
    middle = complex_product(left_map[:, 0], current, "eij,ejk->eik").astype(jnp.bfloat16)
    current = (
        green_free[:, 0].astype(jnp.float32)
        + complex_product(middle, right_map[:, 0], "eij,ejk->eik")
    ).astype(jnp.bfloat16)
    results = [current]
    green = jnp.stack(results, axis=1)
    shape_one = (energies, slabs, orbitals, orbitals)
    padded = with_halo(green, (("energy", 0),), energies)
    real_sum = jnp.zeros(shape_one, jnp.float32)
    imag_sum = jnp.zeros(shape_one, jnp.float32)
    for shift_no in range(screened.shape[0]):
        begin = energies - shift_offsets[shift_no]
        moved = lax.dynamic_slice_in_dim(padded, begin, energies, 0).astype(jnp.float32)
        weight = screened[shift_no].astype(jnp.float32)
        moved_re = moved[:, :, 0]
        moved_im = moved[:, :, 1]
        weight_re = weight[None, :, 0]
        weight_im = weight[None, :, 1]
        real_sum = real_sum + moved_re * weight_re - moved_im * weight_im
        imag_sum = imag_sum + moved_re * weight_im + moved_im * weight_re
    sigma = jnp.stack([-imag_sum, real_sum], axis=2)
    return (green, sigma)


def solution(mesh):
    placed = (
        P("energy", "slab", None, None, None),
        P("slab", None, None, None),
        P(None, "slab", None, None, None),
        P(),
    )
    return jax.shard_map(
        shards,
        mesh=mesh,
        in_specs=placed,
        out_specs=(P("energy", "slab", None, None, None), P("energy", "slab", None, None, None)),
        check_vma=False,
    )
```

profile of v0, /device:TPU:0, one launch (start us, length us, event | category | flops | bytes accessed | tf_op | source)
XLA Modules:
  0.0 40.0 jit_solution(12892405573116479057)
XLA Ops:
  0.6 0.0 copy-start
  0.6 0.0 copy-start.1
  0.7 1.2 %fusion.37 = f32[256,256]{1,0:T(8,128)S(1)} fusion(bf16[1,1,2,256,256]{4,3,2,1,0:T(8,128)(2,1)} %param.6, bf16[1,2,256,256]{3,2,1,0:T(8,128)(2,1)} %param.7), kind=kOutput, calls=%fused_computation.98 | convolution fusion | flops 33554432 | bytes 524288 | tf_op jit(solution)/shard_map/sij,esjk->esik/dot_general | solution.py:50
  1.9 1.2 %fusion.46 = f32[256,256]{1,0:T(8,128)S(1)} fusion(bf16[1,1,2,256,256]{4,3,2,1,0:T(8,128)(2,1)} %param.6, bf16[1,2,256,256]{3,2,1,0:T(8,128)(2,1)} %param.7), kind=kOutput, calls=%fused_computation.107 | convolution fusion | flops 33554432 | bytes 524288 | tf_op jit(solution)/shard_map/sij,esjk->esik/dot_general | solution.py:47
  3.1 1.2 %fusion.42 = f32[256,256]{1,0:T(8,128)S(1)} fusion(bf16[1,2,256,256]{3,2,1,0:T(8,128)(2,1)} %param.7, bf16[1,1,2,256,256]{4,3,2,1,0:T(8,128)(2,1)} %param.6), kind=kOutput, calls=%fused_computation.103 | convolution fusion | flops 33554432 | bytes 524288 | tf_op jit(solution)/shard_map/esij,sjk->esik/dot_general | solution.py:50
  4.3 1.2 %fusion.49 = f32[256,256]{1,0:T(8,128)S(1)} fusion(bf16[1,1,2,256,256]{4,3,2,1,0:T(8,128)(2,1)} %param.6, bf16[1,2,256,256]{3,2,1,0:T(8,128)(2,1)} %param.7), kind=kOutput, calls=%fused_computation.110 | convolution fusion | flops 33554432 | bytes 524288 | tf_op jit(solution)/shard_map/esij,sjk->esik/dot_general | solution.py:47
  5.5 0.0 copy-done
  5.5 2.3 %all_gather.9 = bf16[2,1,2,256,256]{4,3,2,1,0:T(8,128)(2,1)S(1)} all-gather(bf16[1,1,2,256,256]{4,3,2,1,0:T(8,128)(2,1)S(1)} %copy-done), channel_id=1, replica_groups=mesh['energy'=16,'slab'=2] {'slab'}, dimensions={0}, use_global_device_ids=true | all-gather | bytes 786432 | tf_op jit(solution)/shard_map/all_gather | solution.py:10
  7.8 0.0 copy-done.1
  7.8 0.2 fusion.15
  8.0 0.2 fusion.14
  8.3 0.1 copy.9
  8.5 2.2 %all_gather.11 = bf16[2,1,2,256,256]{4,3,2,1,0:T(8,128)(2,1)S(1)} all-gather(bf16[1,1,2,256,256]{4,3,2,1,0:T(8,128)(2,1)S(1)} %copy.9), channel_id=1, replica_groups=mesh['energy'=16,'slab'=2] {'slab'}, dimensions={0}, use_global_device_ids=true | all-gather | bytes 786432 | tf_op jit(solution)/shard_map/all_gather | solution.py:10
  10.6 0.2 fusion.13
  10.9 0.2 fusion.12
  11.1 0.1 copy.8
  11.3 2.2 %all_gather.10 = bf16[2,1,2,256,256]{4,3,2,1,0:T(8,128)(2,1)S(1)} all-gather(bf16[1,1,2,256,256]{4,3,2,1,0:T(8,128)(2,1)S(1)} %copy.8), channel_id=1, replica_groups=mesh['energy'=16,'slab'=2] {'slab'}, dimensions={0}, use_global_device_ids=true | all-gather | bytes 786432 | tf_op jit(solution)/shard_map/all_gather | solution.py:10
  13.5 3.6 %while.14 = (s32[]{:T(128)}, bf16[1,2,256,256]{3,2,1,0:T(8,128)(2,1)S(1)}, s32[]{:T(128)}, bf16[2,1,2,256,256]{4,3,2,1,0:T(8,128)(2,1)S(1)}, bf16[2,1,2,256,256]...) while((s32[]{:T(128)}, ...), condition=%wide.region_1.2_spmd.clone, body=%wide.region_0.1_spmd.clone.sunk | while | flops 269746176 | bytes 7864442 | solution.py:25
  13.5 0.2 fusion.106
  13.7 0.2 fusion.107
  13.9 0.2 fusion.103
  14.1 0.2 fusion.104
  14.3 0.2 fusion.109
  14.5 0.2 fusion.110
  14.7 0.2 fusion.105
  14.9 0.2 fusion.108
  15.1 0.2 fusion.111
  15.3 0.2 fusion.106
  15.5 0.2 fusion.107
  15.7 0.2 fusion.103
  15.9 0.2 fusion.104
  16.1 0.2 fusion.109
  16.3 0.2 fusion.110
  16.5 0.2 fusion.105
  16.7 0.2 fusion.108
  16.9 0.2 fusion.111
  17.0 0.2 fusion.27
  17.3 0.2 fusion.29
  17.5 0.2 fusion.16
  17.7 0.0 copy-start.4
  17.7 0.0 copy-start.2
  17.7 0.2 fusion.22
  18.0 0.2 fusion.20
  18.2 0.2 fusion.17
  18.4 0.2 fusion.10
  18.7 0.2 fusion.11
  18.9 0.1 fusion.18
  19.0 0.0 copy-start.3
  19.0 6.9 %collective-permute-start.1 = (bf16[1,1,2,256,256]{4,3,2,1,0:T(8,128)(2,1)S(1)}, bf16[1,1,2,256,256]{4,3,2,1,0:T(8,128)(2,1)S(1)}, u32[]{:S(2)}, u32[]{:S(2)}) collective-permute-start(bf16[1,1,2,256,256]{4,3,2,1,0:T(8,128)(2,1)S(1)} %fusion.18), channel_id=1, source_target_pairs={{2,0},{4,2},{6,4},{8,6},{10,8},{12,10},{14,12},{16,14},{18,16},{20... | collective-permute-start | bytes 786440 | tf_op jit(solution)/shard_map/ppermute | solution.py:37
  25.9 0.0 collective-permute-start
  25.9 0.0 copy-done.4
  25.9 0.7 %fusion.77 = (s32[1]{0:T(128)}, s32[1]{0:T(128)}, s32[1]{0:T(128)}, s32[1]{0:T(128)}, s32[1]{0:T(128)}, /*index=5*/s32[1]{0:T(128)}, s32[1]{0:T(128)}, s32[1]{0:T(128)}) fusion(s32[8]{0:T(128)S(1)} %copy-done.4), kind=kLoop, calls=%fused_computation.138 | loop fusion | bytes 64 | tf_op jit(solution)/shard_map/slice | solution.py:101
  36.5 0.0 copy-done.2
  36.5 0.4 %bitcast_convert_fusion.7 = (f32[1,2,256,256]{3,2,1,0:T(8,128)S(1)}, f32[1,2,256,256]{3,2,1,0:T(8,128)S(1)}, f32[1,2,256,256]{3,2,1,0:T(8,128)S(1)}, f32[1,2,256...) fusion(bf16[8,1,2,256,256]{4,3,2,1,0:T(8,128)(2,1)S(1)} %copy-d, ...), kind=kLoop, calls=%fused_computation.69 | loop fusion | flops 1048576 | bytes 6291456 | tf_op jit(solution)/shard_map/convert_element_type | solution.py:103
  37.0 0.0 collective-permute-done.1
  37.0 0.6 %collective-permute-done = bf16[1,1,2,256,256]{4,3,2,1,0:T(8,128)(2,1)S(1)} collective-permute-done((bf16[1,1,2,256,256]{4,3,2,1,0:T(8,128)(2,1)S(1)}, bf16[1,1,2,256,256]{4,3,2,1,0:T(8,128)(2,1)S(1)}, u32[]{:S(2)}, u32[]{:S(2)}) %collective-permute-start) | collective-permute-done | bytes 262176 | tf_op jit(solution)/shard_map/ppermute | solution.py:34
  37.5 0.0 copy-done.3
  37.5 0.1 pad_maximum_fusion
  37.6 0.5 %dynamic-slice_convert_fusion = (f32[1,1,2,256,256]{4,3,2,1,0:T(8,128)S(1)}, f32[1,1,2,256,256]{4,3,2,1,0:T(8,128)S(1)}, f32[1,1,2,256,256]{4,3,2,1,0:T(8,128)S(...) fusion(bf16[3,1,2,256,256]{4,3,2,1,0:T(8,128)(2,1)S(1)} %pad_ma, ...), kind=kLoop, calls=%fused_computation.72 | loop fusion | flops 1048576 | bytes 6291488 | tf_op jit(solution)/shard_map/convert_element_type | solution.py:102
  38.1 0.5 %negate_bitcast_fusion = f32[1,1,1,256,256]{4,3,2,1,0:T(8,128)S(1)} fusion(f32[1,1,2,256,256]{4,3,2,1,0:T(8,128)S(1)} %get-tuple-element.168, f32[1,1,2,256,256]{4,3,2,1,0:T(8,128)S(1)} %get-tuple-element.167, f32[1,1,2,256,256]{4,3,2,1,0:T(8,128)S(1)} %get-tuple-element.166, f32[1,1,2,256,256]{4,3,2,1,0:T(8,128)S(1)} %get-tuple-element.165, ...), kind=kLoop, calls=%fused_computation.71 | loop fusion | flops 2097152 | bytes 8650752 | tf_op jit(solution)/shard_map/stack | solution.py:110
  38.7 0.5 %subtract_bitcast_fusion = f32[1,1,1,256,256]{4,3,2,1,0:T(8,128)S(1)} fusion(f32[1,1,2,256,256]{4,3,2,1,0:T(8,128)S(1)} %get-tuple-element.168, f32[1,1,2,256,256]{4,3,2,1,0:T(8,128)S(1)} %get-tuple-element.167, f32[1,1,2,256,256]{4,3,2,1,0:T(8,128)S(1)} %get-tuple-element.166, f32[1,1,2,256,256]{4,3,2,1,0:T(8,128)S(1)} %get-tuple-element.165, ...), kind=kLoop, calls=%fused_computation.70 | loop fusion | flops 2031616 | bytes 8650752 | tf_op jit(solution)/shard_map/stack | solution.py:110
  39.2 0.8 %pad_maximum_fusion.1 = f32[1,1,2,256,256]{4,3,2,1,0:T(8,128)} fusion(f32[1,1,1,256,256]{4,3,2,1,0:T(8,128)S(1)} %subtract_bitcast_fusion, f32[1,1,1,256,256]{4,3,2,1,0:T(8,128)S(1)} %negate_bitcast_fusion), kind=kLoop, calls=%fused_computation.43 | loop fusion | flops 131072 | bytes 1048576 | tf_op jit(solution)/shard_map/stack | solution.py:110
  (7 shorter events, 0.2 us)
Async XLA Ops:
  0.6 4.9 %copy-start = (bf16[1,1,2,256,256]{4,3,2,1,0:T(8,128)(2,1)S(1)}, bf16[1,1,2,256,256]{4,3,2,1,0:T(8,128)(2,1)}, u32[]{:S(2)}) copy-start(bf16[1,1,2,256,256]{4,3,2,1,0:T(8,128)(2,1)} %param.6) | copy-start | bytes 786436
  0.6 7.2 %copy-start.1 = (bf16[1,2,256,256]{3,2,1,0:T(8,128)(2,1)S(1)}, bf16[1,2,256,256]{3,2,1,0:T(8,128)(2,1)}, u32[]{:S(2)}) copy-start(bf16[1,2,256,256]{3,2,1,0:T(8,128)(2,1)} %param.7) | copy-start | bytes 786436
  17.7 8.2 %copy-start.4 = (s32[8]{0:T(128)S(1)}, s32[8]{0:T(128)}, u32[]{:S(2)}) copy-start(s32[8]{0:T(128)} %param.9) | copy-start | bytes 100
  17.7 18.8 %copy-start.2 = (bf16[8,1,2,256,256]{4,3,2,1,0:T(8,128)(2,1)S(1)}, bf16[8,1,2,256,256]{4,3,2,1,0:T(8,128)(2,1)}, u32[]{:S(2)}) copy-start(bf16[8,1,2,256,256]{4,3,2,1,0:T(8,128)(2,1)} %param.8) | copy-start | bytes 6291460
  19.0 18.6 %copy-start.3 = (bf16[1,1,2,256,256]{4,3,2,1,0:T(8,128)(2,1)}, bf16[1,1,2,256,256]{4,3,2,1,0:T(8,128)(2,1)S(1)}, u32[]{:S(2)}) copy-start(bf16[1,1,2,256,256]{4,3,2,1,0:T(8,128)(2,1)S(1)} %fusion.18) | copy-start | bytes 786436
  19.0 18.0 %collective-permute-start.1 = (bf16[1,1,2,256,256]{4,3,2,1,0:T(8,128)(2,1)S(1)}, bf16[1,1,2,256,256]{4,3,2,1,0:T(8,128)(2,1)S(1)}, u32[]{:S(2)}, u32[]{:S(2)}) collective-permute-start(bf16[1,1,2,256,256]{4,3,2,1,0:T(8,128)(2,1)S(1)} %fusion.18), channel_id=1, source_target_pairs={{2,0},{4,2},{6,4},{8,6},{10,8},{12,10},{14,12},{16,14},{18,16},{20... | collective-permute-start | bytes 786440 | tf_op jit(solution)/shard_map/ppermute | solution.py:37
  25.9 11.7 %collective-permute-start = (bf16[1,1,2,256,256]{4,3,2,1,0:T(8,128)(2,1)S(1)}, bf16[1,1,2,256,256]{4,3,2,1,0:T(8,128)(2,1)S(1)}, u32[]{:S(2)}, u32[]{:S(2)}) collective-permute-start(bf16[1,1,2,256,256]{4,3,2,1,0:T(8,128)(2,1)S(1)} %fusion.18), channel_id=1, source_target_pairs={{0,2},{2,4},{4,6},{6,8},{8,10},{10,12},{12,14},{14,16},{16,18},{18... | collective-permute-start | bytes 786440 | tf_op jit(solution)/shard_map/ppermute | solution.py:34
where the time goes:
time: 40.4 us; the launch traced here: 40 us
  between operations  10.8 us (27%)
  matrix products  10.4 us (26%)
  starting transfers between devices  6.9 us (17%)
  blocking collectives  6.66 us (16%)
  other arithmetic  3.41 us (8%)
  local copies, waits for them, and re-layouts  1.07 us (3%)
  waiting for transfers between devices  0.57 us (1%)
    ppermute x1, starting transfers between devices, with_halo(): lax.ppermute(lax.slice_in_dim(block, 0, width, axis=dim), axis, backward)  6.9 us
    all_gather x3, blocking collectives, prefix(): lax.all_gather(part.astype(kind), axis)  6.66 us
    dot_general x8, matrix products, complex_product(): jnp.einsum(form, first_re, second_im, preferred_element_type=jnp.float32)  3.59 us
    dot_general x8, matrix products, complex_product(): jnp.einsum(form, first_re, second_re, preferred_element_type=jnp.float32)  3.54 us
    another operation x3, other arithmetic, shards(): sigma = jnp.stack([-imag_sum, real_sum], axis=2)  1.92 us
    dot_general x8, matrix products, complex_product(): jnp.einsum(form, first_im, second_re, preferred_element_type=jnp.float32)  1.65 us
    dot_general x8, matrix products, complex_product(): jnp.einsum(form, first_im, second_im, preferred_element_type=jnp.float32)  1.65 us
  transfers between devices with their start and end apart: 2, of which 1 were waited for; matrix products, arithmetic and copies ran while one was open for 3% of the time, Pallas kernels for 0%

commit v1 on v0

v1 whole, which is shorter than its diff:
```python
import functools

import jax
import jax.numpy as jnp
from jax import lax
from jax.experimental import pallas as pl
from jax.experimental.pallas import tpu as pltpu
from jax.sharding import PartitionSpec as P


VMEM = pl.BlockSpec(memory_space=pltpu.VMEM)
HBM = pl.BlockSpec(memory_space=pltpu.HBM)
SMEM = pl.BlockSpec(memory_space=pltpu.SMEM)


def dot(a, b):
    return jnp.dot(a, b, preferred_element_type=jnp.float32)


def dot_t(a, b):
    return lax.dot_general(a, b, (((0,), (0,)), ((), ())), preferred_element_type=jnp.float32)


def times(a, b):
    return dot(a[0], b[0]) - dot(a[1], b[1]), dot(a[0], b[1]) + dot(a[1], b[0])


def load_kernel(slab_ref, free_hbm, coupling_hbm, free_ref, coupling_ref, left_ref, right_ref, sems):
    copies = [
        pltpu.make_async_copy(free_hbm, free_ref, sems.at[0]),
        pltpu.make_async_copy(coupling_hbm, coupling_ref, sems.at[1]),
    ]
    for copy in copies:
        copy.start()
    for copy in copies:
        copy.wait()
    maps_kernel(slab_ref, free_ref, coupling_ref, left_ref, right_ref)


def maps_kernel(slab_ref, free_ref, coupling_ref, left_ref, right_ref):
    @pl.when(slab_ref[0] > 0)
    def _():
        free = free_ref[0], free_ref[1]
        coupling = coupling_ref[0], coupling_ref[1]
        left = times(free, coupling)
        left_ref[0] = left[0].astype(left_ref.dtype)
        left_ref[1] = left[1].astype(left_ref.dtype)
        right_re = dot_t(coupling[0], free[0]) + dot_t(coupling[1], free[1])
        right_im = dot_t(coupling[0], free[1]) - dot_t(coupling[1], free[0])
        right_ref[0] = right_re.astype(right_ref.dtype)
        right_ref[1] = right_im.astype(right_ref.dtype)


def advance_kernel(step, slab_ref, before_ref, now_ref, left_ref, right_ref, green_ref):
    @pl.when(slab_ref[0] == step)
    def _():
        middle = times((left_ref[0], left_ref[1]), (before_ref[0], before_ref[1]))
        middle = middle[0].astype(jnp.bfloat16), middle[1].astype(jnp.bfloat16)
        added = times(middle, (right_ref[0], right_ref[1]))
        for part in range(2):
            fresh = now_ref[part].astype(jnp.float32) + added[part]
            green_ref[part] = fresh.astype(green_ref.dtype)

    @pl.when(slab_ref[0] != step)
    def _():
        green_ref[...] = now_ref[...]


def weights_kernel(place_ref, screened_ref, total_ref):
    total_ref[...] = jnp.zeros_like(total_ref)
    for shift in range(screened_ref.shape[0]):
        at = place_ref[shift]
        total_ref[at] += screened_ref[shift].astype(jnp.float32)


def add_products(pairs):
    real, imag = None, None
    for green, weight in pairs:
        green_re, green_im = green[0].astype(jnp.float32), green[1].astype(jnp.float32)
        one = green_re * weight[0] - green_im * weight[1]
        two = green_re * weight[1] + green_im * weight[0]
        real = one if real is None else real + one
        imag = two if imag is None else imag + two
    return real, imag


def near_kernel(own_ref, near_ref, total_ref, sum_ref):
    real, imag = add_products(
        (((own_ref[0], own_ref[1]), (total_ref[0, 0], total_ref[0, 1])),
         ((near_ref[0], near_ref[1]), (total_ref[1, 0], total_ref[1, 1])))
    )
    sum_ref[0] = -imag
    sum_ref[1] = real


def far_kernel(sum_ref, far_ref, total_ref, sigma_ref):
    real, imag = add_products((((far_ref[0], far_ref[1]), (total_ref[2, 0], total_ref[2, 1])),))
    sigma_ref[0] = sum_ref[0] - imag
    sigma_ref[1] = sum_ref[1] + real


PARAMS = pltpu.CompilerParams(vmem_limit_bytes=16 * 2**20)


def in_vmem(shape, dtype):
    return pltpu.VMEM(shape, dtype)


def shards(green_free, coupling, screened, shift_offsets):
    energies, slabs, parts, orbitals, _ = green_free.shape
    assert energies == 1 and slabs == 1
    count, segments = lax.axis_size("energy"), lax.axis_size("slab")
    block = (parts, orbitals, orbitals)
    free = green_free.reshape(block)
    coupled = coupling.reshape(block)
    weight = screened.reshape((screened.shape[0],) + block)
    slab = lax.axis_index("slab").astype(jnp.int32).reshape(1)

    if count % 2 == 0:
        first_pairs = [(e, (e + 1 if e % 2 else e - 1) % count) for e in range(count)]
        second_pairs = [(e, e ^ 1) for e in range(count)]
        toward = 1 - 2 * (lax.axis_index("energy") % 2)
    else:
        first_pairs = [(e, (e - 1) % count) for e in range(count)]
        second_pairs = [(e, (e + 1) % count) for e in range(count)]
        toward = -1
    place = jnp.where(shift_offsets == 0, 0, jnp.where(shift_offsets == toward, 1, 2))
    ring = [(s, (s + 1) % segments) for s in range(segments)]

    product = 8 * orbitals**3
    size = 2 * parts * orbitals * orbitals
    small = in_vmem(block, jnp.bfloat16)

    def cost(flops, arrays):
        return pl.CostEstimate(flops=flops, bytes_accessed=arrays * size, transcendentals=0)

    def swap(part):
        return lax.ppermute(part, "slab", ring)

    def advance(step, before, now, left, right):
        return pl.pallas_call(
            functools.partial(advance_kernel, step),
            out_shape=small,
            in_specs=[SMEM] + [VMEM] * 4,
            out_specs=VMEM,
            cost_estimate=cost(2 * product, 5),
            compiler_params=PARAMS,
        )(slab, before, now, left, right)

    before = swap(free)
    first_free = lax.ppermute(free, "energy", first_pairs)
    own, coupled, left, right = pl.pallas_call(
        load_kernel,
        out_shape=(small,) * 4,
        in_specs=[SMEM, HBM, HBM],
        out_specs=[VMEM] * 4,
        scratch_shapes=[pltpu.SemaphoreType.DMA((2,))],
        cost_estimate=cost(2 * product, 6),
        compiler_params=PARAMS,
    )(slab, free, coupled)
    green = own
    for step in range(1, segments):
        green = advance(step, before, green, left, right)
        if step < segments - 1:
            before = swap(green)
    second = lax.ppermute(green, "energy", second_pairs)
    total = pl.pallas_call(
        weights_kernel,
        out_shape=in_vmem((3,) + block, jnp.float32),
        in_specs=[SMEM, VMEM],
        out_specs=VMEM,
        cost_estimate=cost(0, screened.shape[0] + 6),
        compiler_params=PARAMS,
    )(place, weight)
    first = first_free
    before = swap(first)
    left, right = pl.pallas_call(
        maps_kernel,
        out_shape=(small,) * 2,
        in_specs=[SMEM, VMEM, VMEM],
        out_specs=[VMEM, VMEM],
        cost_estimate=cost(2 * product, 4),
        compiler_params=PARAMS,
    )(slab, first, coupled)
    for step in range(1, segments):
        first = advance(step, before, first, left, right)
        if step < segments - 1:
            before = swap(first)
    partial = pl.pallas_call(
        near_kernel,
        out_shape=in_vmem(block, jnp.float32),
        in_specs=[VMEM] * 3,
        out_specs=VMEM,
        cost_estimate=cost(0, 10),
        compiler_params=PARAMS,
    )(green, first, total)
    sigma = pl.pallas_call(
        far_kernel,
        out_shape=jax.ShapeDtypeStruct(block, jnp.float32),
        in_specs=[VMEM] * 3,
        out_specs=VMEM,
        cost_estimate=cost(0, 10),
        compiler_params=PARAMS,
    )(partial, second, total)
    shape = (energies, slabs) + block
    return green.reshape(shape), sigma.reshape(shape)


def solution(mesh):
    placed = (
        P("energy", "slab", None, None, None),
        P("slab", None, None, None),
        P(None, "slab", None, None, None),
        P(),
    )
    return jax.shard_map(
        shards,
        mesh=mesh,
        in_specs=placed,
        out_specs=(P("energy", "slab", None, None, None), P("energy", "slab", None, None, None)),
        check_vma=False,
    )
```

time: 40.4 us -> 24.5 us (0.61)
  waiting for transfers between devices: 0.57 us -> 11.6 us
  matrix products: 10.4 us -> 0 us
  between operations: 10.8 us -> 0.7 us
  blocking collectives: 6.66 us -> 0 us
  other arithmetic: 3.41 us -> 0.01 us
  Pallas kernels: 0 us -> 2.33 us
  local copies, waits for them, and re-layouts: 1.07 us -> 2.61 us
    ppermute x2 -> x4, waiting for transfers between devices: 0.57 us -> 11.6 us  [the longest x1 7.03 us: shards(): second = lax.ppermute(green, 'energy', second_pairs)]
    dot_general x32 -> x0, matrix products: 10.4 us -> none  [the longest x8 3.59 us: complex_product(): jnp.einsum(form, first_re, second_im, preferred_element_type=jnp.float32)]
    all_gather x3 -> x0, blocking collectives: 6.66 us -> none  [prefix(): lax.all_gather(part.astype(kind), axis)]
    unnamed x10 -> x9, local copies, waits for them, and re-layouts: 0.03 us -> 2.61 us
    pallas_call x0 -> x7, Pallas kernels: none -> 2.33 us  [the longest x1 1.1 us: shards(): pl.pallas_call(weights_kernel, out_shape=in_vmem((3,) + block, jnp.float3...]
    another operation x5 -> x0, other arithmetic: 1.98 us -> none  [the longest x3 1.92 us: shards(): sigma = jnp.stack([-imag_sum, real_sum], axis=2)]
    convert_element_type x3 -> x0, other arithmetic: 0.97 us -> none  [the longest x1 0.46 us: shards(): lax.dynamic_slice_in_dim(padded, begin, energies, 0).astype(jnp.float32)]
    slice x1 -> x0, local copies, waits for them, and re-layouts: 0.68 us -> none  [shards(): begin = energies - shift_offsets[shift_no]]
  transfers between devices with their start and end apart: 2 -> 4, of which waited for: 1 -> 2; matrix products, arithmetic and copies ran while one was open for 3% -> 3% of each run, Pallas kernels for 0% -> 6%
where the time goes in v1:
time: 24.5 us; the launch traced here: 24.3 us
  waiting for transfers between devices  11.6 us (47%)
  starting transfers between devices  7.1 us (29%)
  local copies, waits for them, and re-layouts  2.61 us (11%)
  Pallas kernels  2.33 us (10%)
  between operations  0.7 us (3%)
    ppermute x1, waiting for transfers between devices, shards(): second = lax.ppermute(green, 'energy', second_pairs)  7.03 us
    ppermute x1, starting transfers between devices, shards(): first_free = lax.ppermute(free, 'energy', first_pairs)  7.02 us
    ppermute x1, waiting for transfers between devices, shards(): first_free = lax.ppermute(free, 'energy', first_pairs)  4.54 us
    unnamed x9, local copies, waits for them, and re-layouts  2.61 us
    pallas_call x1, Pallas kernels, shards(): pl.pallas_call(weights_kernel, out_shape=in_vmem((3,) + block, jnp.float3...  1.1 us
    pallas_call x1, Pallas kernels, shards(): pl.pallas_call(far_kernel, out_shape=jax.ShapeDtypeStruct(block, jnp.floa...  0.92 us
  transfers between devices with their start and end apart: 4, of which 2 were waited for; matrix products, arithmetic and copies ran while one was open for 3% of the time, Pallas kernels for 6%

profile of v1, /device:TPU:0, one launch (start us, length us, event | category | flops | bytes accessed | tf_op | source)
XLA Modules:
  0.0 24.3 jit_solution(16168881537310131649)
XLA Ops:
  0.6 0.0 copy-start
  0.6 7.0 %collective-permute-start.1 = (bf16[2,256,256]{2,1,0:T(8,128)(2,1)}, bf16[2,256,256]{2,1,0:T(8,128)(2,1)S(1)}, u32[]{:S(2)}, u32[]{:S(2)}) collective-permute-start(bf16[2,256,256]{2,1,0:T(8,128)(2,1)} %bitcast.9), channel_id=1, source_target_pairs={{0,30},{2,4},{4,2},{6,8},{8,6},{10,12},{12,10},{14,16},{16,14},{18... | collective-permute-start | bytes 786440 | tf_op jit(solution)/shard_map/ppermute | solution.py:151
  7.7 0.0 collective-permute-start
  7.7 0.0 copy-start.1
  7.7 0.9 %copy-done.1 = bf16[1,2,256,256]{3,2,1,0:T(8,128)(2,1)S(1)} copy-done((bf16[1,2,256,256]{3,2,1,0:T(8,128)(2,1)S(1)}, bf16[1,2,256,256]{3,2,1,0:T(8,128)(2,1)}, u32[]{:S(2)}) %copy-start.1) | copy-done | bytes 262168
  8.6 0.0 copy-start.2
  8.6 0.9 %copy-done.2 = bf16[1,1,2,256,256]{4,3,2,1,0:T(8,128)(2,1)S(1)} copy-done((bf16[1,1,2,256,256]{4,3,2,1,0:T(8,128)(2,1)S(1)}, bf16[1,1,2,256,256]{4,3,2,1,0:T(8,128)(2,1)}, u32[]{:S(2)}) %copy-start.2) | copy-done | bytes 262168
  9.6 0.0 copy-start.3
  9.6 0.1 shard_map.59
  9.6 4.5 %collective-permute-done.1.free_ref.now_ref = bf16[2,256,256]{2,1,0:T(8,128)(2,1)S(1)} collective-permute-done((bf16[2,256,256]{2,1,0:T(8,128)(2,1)}, bf16[2,256,256]{2,1,0:T(8,128)(2,1)S(1)}, u32[]{:S(2)}, u32[]{:S(2)}) %collective-permute-start.1) | collective-permute-done | bytes 262176 | tf_op jit(solution)/shard_map/ppermute | solution.py:151
  14.2 0.0 collective-permute-start.2
  14.2 0.0 collective-permute-done.before_ref
  14.2 0.1 collective-permute-start.3
  14.3 0.0 copy-done.3
  14.3 0.0 copy-done
  14.3 1.1 %shard_map.63.total_ref = f32[3,2,256,256]{3,2,1,0:T(8,128)S(1)} custom-call(s32[8]{0:T(128)S(1)} %compare_select_fusion.1.place_ref, bf16[8,2,256,256]{3,2,1,0:T(8,128)(2,1)S(1)} %bitcast.7), custom_call_target="tpu_custom_call" | custom-call | bytes 3670016 | tf_op jit(solution)/shard_map/pallas_call | solution.py:167
  15.4 0.7 %copy.6 = bf16[1,1,2,256,256]{4,3,2,1,0:T(8,128)(2,1)} copy(bf16[1,1,2,256,256]{4,3,2,1,0:T(8,128)(2,1)S(1)} %bitcast.6) | data formatting | bytes 524288
  16.1 0.0 collective-permute-done.2.before_ref
  16.2 0.2 shard_map.64.sum_ref
  16.4 7.0 %collective-permute-done.3.far_ref = bf16[2,256,256]{2,1,0:T(8,128)(2,1)S(1)} collective-permute-done((bf16[2,256,256]{2,1,0:T(8,128)(2,1)S(1)}, bf16[2,256,256]{2,1,0:T(8,128)(2,1)S(1)}, u32[]{:S(2)}, u32[]{:S(2)}) %collective-permute-start.3) | collective-permute-done | bytes 262176 | tf_op jit(solution)/shard_map/ppermute | solution.py:166
  23.4 0.9 %shard_map.65 = f32[2,256,256]{2,1,0:T(8,128)} custom-call(f32[2,256,256]{2,1,0:T(8,128)S(1)} %shard_map.64.sum_ref, bf16[2,256,256]{2,1,0:T(8,128)(2,1)S(1)} %collective-permute-done.3.far_ref, f32[3,2,256,256]{3,2,1,0:T(8,128)S(1)} %shard_map.63.total_ref), custom_call_target="tpu_custom_call" | custom-call | bytes 2621440 | tf_op jit(solution)/shard_map/pallas_call | solution.py:197
  (4 shorter events, 0.0 us)
Async XLA Ops:
  0.6 13.7 %copy-start = (bf16[8,1,2,256,256]{4,3,2,1,0:T(8,128)(2,1)S(1)}, bf16[8,1,2,256,256]{4,3,2,1,0:T(8,128)(2,1)}, u32[]{:S(2)}) copy-start(bf16[8,1,2,256,256]{4,3,2,1,0:T(8,128)(2,1)} %param.6) | copy-start | bytes 6291460
  0.6 13.5 %collective-permute-start.1 = (bf16[2,256,256]{2,1,0:T(8,128)(2,1)}, bf16[2,256,256]{2,1,0:T(8,128)(2,1)S(1)}, u32[]{:S(2)}, u32[]{:S(2)}) collective-permute-start(bf16[2,256,256]{2,1,0:T(8,128)(2,1)} %bitcast.9), channel_id=1, source_target_pairs={{0,30},{2,4},{4,2},{6,8},{8,6},{10,12},{12,10},{14,16},{16,14},{18... | collective-permute-start | bytes 786440 | tf_op jit(solution)/shard_map/ppermute | solution.py:151
  7.7 6.5 %collective-permute-start = (bf16[2,256,256]{2,1,0:T(8,128)(2,1)}, bf16[2,256,256]{2,1,0:T(8,128)(2,1)S(1)}, u32[]{:S(2)}, u32[]{:S(2)}) collective-permute-start(bf16[2,256,256]{2,1,0:T(8,128)(2,1)} %bitcast.10), channel_id=1, source_target_pairs={{0,1},{1,0},{2,3},{3,2},{4,5},{5,4},{6,7},{7,6},{8,9},{9,8},{10,11... | collective-permute-start | bytes 786440 | tf_op jit(solution)/shard_map/ppermute | solution.py:138
  7.7 1.0 %copy-start.1 = (bf16[1,2,256,256]{3,2,1,0:T(8,128)(2,1)S(1)}, bf16[1,2,256,256]{3,2,1,0:T(8,128)(2,1)}, u32[]{:S(2)}) copy-start(bf16[1,2,256,256]{3,2,1,0:T(8,128)(2,1)} %param.5) | copy-start | bytes 786436
  8.6 0.9 %copy-start.2 = (bf16[1,1,2,256,256]{4,3,2,1,0:T(8,128)(2,1)S(1)}, bf16[1,1,2,256,256]{4,3,2,1,0:T(8,128)(2,1)}, u32[]{:S(2)}) copy-start(bf16[1,1,2,256,256]{4,3,2,1,0:T(8,128)(2,1)} %param.4) | copy-start | bytes 786436
  9.6 4.7 %copy-start.3 = (s32[8]{0:T(128)S(1)}, s32[8]{0:T(128)}, u32[]{:S(2)}) copy-start(s32[8]{0:T(128)} %param.7) | copy-start | bytes 100
  14.2 2.0 %collective-permute-start.2 = (bf16[2,256,256]{2,1,0:T(8,128)(2,1)S(1)}, bf16[2,256,256]{2,1,0:T(8,128)(2,1)S(1)}, u32[]{:S(2)}, u32[]{:S(2)}) collective-permute-start(bf16[2,256,256]{2,1,0:T(8,128)(2,1)S(1)} %collective-permute-done.1.free_ref.now_ref), channel_id=1, source_target_pairs={{0,1},{1,0},{2,3},{3,2},{4,5},{5,4},{6,7},{7,6},{8,9},{9,8},{10,11... | collective-permute-start | bytes 786440 | tf_op jit(solution)/shard_map/ppermute | solution.py:138
  14.2 9.2 %collective-permute-start.3 = (bf16[2,256,256]{2,1,0:T(8,128)(2,1)S(1)}, bf16[2,256,256]{2,1,0:T(8,128)(2,1)S(1)}, u32[]{:S(2)}, u32[]{:S(2)}) collective-permute-start(bf16[2,256,256]{2,1,0:T(8,128)(2,1)S(1)} %shard_map.60.own_ref), channel_id=1, source_target_pairs={{0,2},{2,0},{4,6},{6,4},{8,10},{10,8},{12,14},{14,12},{16,18},{18,... | collective-permute-start | bytes 786440 | tf_op jit(solution)/shard_map/ppermute | solution.py:166

commit v2 on v1

--- a/solution.py
+++ b/solution.py
@@ -25,7 +25,7 @@
     return dot(a[0], b[0]) - dot(a[1], b[1]), dot(a[0], b[1]) + dot(a[1], b[0])
 
 
-def load_kernel(slab_ref, free_hbm, coupling_hbm, free_ref, coupling_ref, left_ref, right_ref, sems):
+def load_kernel(slab_ref, free_hbm, coupling_hbm, free_ref, left_ref, right_ref, coupling_ref, sems):
     copies = [
         pltpu.make_async_copy(free_hbm, free_ref, sems.at[0]),
         pltpu.make_async_copy(coupling_hbm, coupling_ref, sems.at[1]),
@@ -34,10 +34,10 @@
         copy.start()
     for copy in copies:
         copy.wait()
-    maps_kernel(slab_ref, free_ref, coupling_ref, left_ref, right_ref)
-
-
-def maps_kernel(slab_ref, free_ref, coupling_ref, left_ref, right_ref):
+    write_maps(slab_ref, free_ref, coupling_ref, left_ref, right_ref)
+
+
+def write_maps(slab_ref, free_ref, coupling_ref, left_ref, right_ref):
     @pl.when(slab_ref[0] > 0)
     def _():
         free = free_ref[0], free_ref[1]
@@ -66,11 +66,15 @@
         green_ref[...] = now_ref[...]
 
 
-def weights_kernel(place_ref, screened_ref, total_ref):
+def weights_kernel(offset_ref, toward_ref, screened_ref, green_ref, total_ref, green_hbm, sem):
+    copy = pltpu.make_async_copy(green_ref, green_hbm, sem)
+    copy.start()
     total_ref[...] = jnp.zeros_like(total_ref)
     for shift in range(screened_ref.shape[0]):
-        at = place_ref[shift]
+        offset = offset_ref[shift]
+        at = jnp.where(offset == 0, 0, jnp.where(offset == toward_ref[0], 1, 2))
         total_ref[at] += screened_ref[shift].astype(jnp.float32)
+    copy.wait()
 
 
 def add_products(pairs):
@@ -84,22 +88,57 @@
     return real, imag
 
 
-def near_kernel(own_ref, near_ref, total_ref, sum_ref):
-    real, imag = add_products(
-        (((own_ref[0], own_ref[1]), (total_ref[0, 0], total_ref[0, 1])),
-         ((near_ref[0], near_ref[1]), (total_ref[1, 0], total_ref[1, 1])))
-    )
-    sum_ref[0] = -imag
-    sum_ref[1] = real
-
-
-def far_kernel(sum_ref, far_ref, total_ref, sigma_ref):
-    real, imag = add_products((((far_ref[0], far_ref[1]), (total_ref[2, 0], total_ref[2, 1])),))
-    sigma_ref[0] = sum_ref[0] - imag
-    sigma_ref[1] = sum_ref[1] + real
+def pick_kernel(slab_ref, one_ref, two_ref, out_ref):
+    @pl.when(slab_ref[0] == 0)
+    def _():
+        out_ref[...] = one_ref[...]
+
+    @pl.when(slab_ref[0] != 0)
+    def _():
+        out_ref[...] = two_ref[...]
+
+
+def partial_kernel(slab_ref, own_ref, one_ref, two_ref, total_ref, sum_ref):
+    def write(other_ref):
+        real, imag = add_products(
+            (((own_ref[0], own_ref[1]), (total_ref[0, 0], total_ref[0, 1])),
+             ((other_ref[0], other_ref[1]), (total_ref[1, 0], total_ref[1, 1])))
+        )
+        sum_ref[0] = -imag
+        sum_ref[1] = real
+
+    @pl.when(slab_ref[0] == 0)
+    def _():
+        write(one_ref)
+
+    @pl.when(slab_ref[0] != 0)
+    def _():
+        write(two_ref)
+
+
+CHUNKS = 4
+
+
+def far_kernel(sum_ref, far_ref, total_ref, sigma_hbm, sigma_ref, sems):
+    rows = far_ref.shape[1] // CHUNKS
+    copies = []
+    for chunk in range(CHUNKS):
+        at = pl.ds(chunk * rows, rows)
+        real, imag = add_products((((far_ref[0, at], far_ref[1, at]), (total_ref[2, 0, at], total_ref[2, 1, at])),))
+        sigma_ref[0, at] = sum_ref[0, at] - imag
+        sigma_ref[1, at] = sum_ref[1, at] + real
+        for part in range(2):
+            copies.append(pltpu.make_async_copy(sigma_ref.at[part, at], sigma_hbm.at[part, at], sems.at[chunk, part]))
+            copies[-1].start()
+    for copy in copies:
+        copy.wait()
 
 
 PARAMS = pltpu.CompilerParams(vmem_limit_bytes=16 * 2**20)
+
+
+def in_hbm(array):
+    return pltpu.with_memory_space_constraint(array, pltpu.HBM)
 
 
 def in_vmem(shape, dtype):
@@ -116,15 +155,27 @@
     weight = screened.reshape((screened.shape[0],) + block)
     slab = lax.axis_index("slab").astype(jnp.int32).reshape(1)
 
+    after = [(e + 1) % count for e in range(count)]
     if count % 2 == 0:
-        first_pairs = [(e, (e + 1 if e % 2 else e - 1) % count) for e in range(count)]
-        second_pairs = [(e, e ^ 1) for e in range(count)]
-        toward = 1 - 2 * (lax.axis_index("energy") % 2)
+        near = [e ^ 1 for e in range(count)]
+        far = [(e + 1 if e % 2 else e - 1) % count for e in range(count)]
+        onward = [(e - 2 if e % 2 else e + 2) % count for e in range(count)]
+        toward_near = 2 * (lax.axis_index("energy") % 2) - 1
     else:
-        first_pairs = [(e, (e - 1) % count) for e in range(count)]
-        second_pairs = [(e, (e + 1) % count) for e in range(count)]
-        toward = -1
-    place = jnp.where(shift_offsets == 0, 0, jnp.where(shift_offsets == toward, 1, 2))
+        near = after
+        far = [(e - 1) % count for e in range(count)]
+        onward = [(e - 2) % count for e in range(count)]
+        toward_near = 1
+    idle = [e ^ 2 for e in range(count)] if count % 4 == 0 else after
+    toward = jnp.where(slab == 0, toward_near, -toward_near).astype(jnp.int32)
+
+    def exchange(part, base, others):
+        pairs = []
+        for e in range(count):
+            for s in range(segments):
+                pairs.append((e * segments + s, (others if s else base)[e] * segments + s))
+        return lax.ppermute(part, ("energy", "slab"), pairs)
+
     ring = [(s, (s + 1) % segments) for s in range(segments)]
 
     product = 8 * orbitals**3
@@ -148,62 +199,59 @@
         )(slab, before, now, left, right)
 
     before = swap(free)
-    first_free = lax.ppermute(free, "energy", first_pairs)
-    own, coupled, left, right = pl.pallas_call(
+    first = exchange(free, near, idle)
+    own, left, right = pl.pallas_call(
         load_kernel,
-        out_shape=(small,) * 4,
+        out_shape=(small,) * 3,
         in_specs=[SMEM, HBM, HBM],
-        out_specs=[VMEM] * 4,
-        scratch_shapes=[pltpu.SemaphoreType.DMA((2,))],
+        out_specs=[VMEM] * 3,
+        scratch_shapes=[small, pltpu.SemaphoreType.DMA((2,))],
         cost_estimate=cost(2 * product, 6),
         compiler_params=PARAMS,
-    )(slab, free, coupled)
+    )(slab, in_hbm(free), in_hbm(coupled))
     green = own
     for step in range(1, segments):
         green = advance(step, before, green, left, right)
         if step < segments - 1:
             before = swap(green)
-    second = lax.ppermute(green, "energy", second_pairs)
-    total = pl.pallas_call(
+    second = exchange(green, idle, far)
+    payload = pl.pallas_call(
+        pick_kernel,
+        out_shape=small,
+        in_specs=[SMEM, VMEM, VMEM],
+        out_specs=VMEM,
+        cost_estimate=cost(0, 3),
+        compiler_params=PARAMS,
+    )(slab, first, green)
+    third = exchange(payload, onward, near)
+    total, green_out = pl.pallas_call(
         weights_kernel,
-        out_shape=in_vmem((3,) + block, jnp.float32),
-        in_specs=[SMEM, VMEM],
-        out_specs=VMEM,
+        out_shape=(in_vmem((3,) + block, jnp.float32), jax.ShapeDtypeStruct(block, jnp.bfloat16)),
+        in_specs=[SMEM, SMEM, VMEM, VMEM],
+        out_specs=[VMEM, HBM],
+        scratch_shapes=[pltpu.SemaphoreType.DMA],
         cost_estimate=cost(0, screened.shape[0] + 6),
         compiler_params=PARAMS,
-    )(place, weight)
-    first = first_free
-    before = swap(first)
-    left, right = pl.pallas_call(
-        maps_kernel,
-        out_shape=(small,) * 2,
-        in_specs=[SMEM, VMEM, VMEM],
-        out_specs=[VMEM, VMEM],
-        cost_estimate=cost(2 * product, 4),
-        compiler_params=PARAMS,
-    )(slab, first, coupled)
-    for step in range(1, segments):
-        first = advance(step, before, first, left, right)
-        if step < segments - 1:
-            before = swap(first)
+    )(shift_offsets, toward, weight, green)
     partial = pl.pallas_call(
-        near_kernel,
+        partial_kernel,
         out_shape=in_vmem(block, jnp.float32),
-        in_specs=[VMEM] * 3,
+        in_specs=[SMEM] + [VMEM] * 4,
         out_specs=VMEM,
         cost_estimate=cost(0, 10),
         compiler_params=PARAMS,
-    )(green, first, total)
+    )(slab, green, first, second, total)
     sigma = pl.pallas_call(
         far_kernel,
         out_shape=jax.ShapeDtypeStruct(block, jnp.float32),
         in_specs=[VMEM] * 3,
-        out_specs=VMEM,
+        out_specs=HBM,
+        scratch_shapes=[in_vmem(block, jnp.float32), pltpu.SemaphoreType.DMA((CHUNKS, 2))],
         cost_estimate=cost(0, 10),
         compiler_params=PARAMS,
-    )(partial, second, total)
+    )(partial, third, total)
     shape = (energies, slabs) + block
-    return green.reshape(shape), sigma.reshape(shape)
+    return green_out.reshape(shape), sigma.reshape(shape)
 
 
 def solution(mesh):

time: 24.5 us -> 19 us (0.78)
  waiting for transfers between devices: 11.6 us -> 7.87 us
  local copies, waits for them, and re-layouts: 2.61 us -> 0.01 us
  Pallas kernels: 2.33 us -> 3.47 us
  starting transfers between devices: 7.1 us -> 6.8 us
    ppermute x2 -> x3, waiting for transfers between devices: 11.6 us -> 7.87 us  [exchange(): return lax.ppermute(part, ('energy', 'slab'), pairs)]
    unnamed x9 -> x4, local copies, waits for them, and re-layouts: 2.61 us -> 0.01 us
    pallas_call x4, Pallas kernels: 1.37 us -> 2.55 us  [the longest x1 1.25 us: shards(): pl.pallas_call(weights_kernel, out_shape=(in_vmem((3,) + block, jnp.float...]
    ppermute x2 -> x3, starting transfers between devices: 7.1 us -> 6.24 us  [exchange(): return lax.ppermute(part, ('energy', 'slab'), pairs)]
    ppermute x2 -> x1, starting transfers between devices: 0.01 us -> 0.56 us  [swap(): return lax.ppermute(part, 'slab', ring)]
  transfers between devices with their start and end apart: 4 -> 4, of which waited for: 2 -> 3; matrix products, arithmetic and copies ran while one was open for 3% -> 0% of each run, Pallas kernels for 6% -> 14%
where the time goes in v2:
time: 19 us; the launch traced here: 18.8 us
  waiting for transfers between devices  7.87 us (41%)
  starting transfers between devices  6.8 us (36%)
  Pallas kernels  3.47 us (18%)
  between operations  0.7 us (4%)
    ppermute x3, waiting for transfers between devices, exchange(): return lax.ppermute(part, ('energy', 'slab'), pairs)  7.87 us
    ppermute x3, starting transfers between devices, exchange(): return lax.ppermute(part, ('energy', 'slab'), pairs)  6.24 us
    pallas_call x1, Pallas kernels, shards(): pl.pallas_call(weights_kernel, out_shape=(in_vmem((3,) + block, jnp.float...  1.25 us
    pallas_call x1, Pallas kernels, shards(): pl.pallas_call(load_kernel, out_shape=(small,) * 3, in_specs=[SMEM, HBM,...  1.04 us
    pallas_call x1, Pallas kernels, shards(): pl.pallas_call(far_kernel, out_shape=jax.ShapeDtypeStruct(block, jnp.floa...  0.88 us
    ppermute x1, starting transfers between devices, swap(): return lax.ppermute(part, 'slab', ring)  0.56 us
  transfers between devices with their start and end apart: 4, of which 3 were waited for; matrix products, arithmetic and copies ran while one was open for 0% of the time, Pallas kernels for 14%

profile of v2, /device:TPU:0, one launch (start us, length us, event | category | flops | bytes accessed | tf_op | source)
XLA Modules:
  0.0 18.8 jit_solution(3961925853022595751)
XLA Ops:
  0.6 0.0 copy-start.1
  0.6 0.0 copy-start
  0.7 0.6 %collective-permute-start = (bf16[2,256,256]{2,1,0:T(8,128)(2,1)}, bf16[2,256,256]{2,1,0:T(8,128)(2,1)S(1)}, u32[]{:S(2)}, u32[]{:S(2)}) collective-permute-start(bf16[2,256,256]{2,1,0:T(8,128)(2,1)} %bitcast.11), channel_id=1, source_target_pairs={{0,1},{1,0},{2,3},{3,2},{4,5},{5,4},{6,7},{7,6},{8,9},{9,8},{10,11... | collective-permute-start | bytes 786440 | tf_op jit(solution)/shard_map/ppermute | solution.py:189
  1.2 2.6 %collective-permute-start.1 = (bf16[2,256,256]{2,1,0:T(8,128)(2,1)}, bf16[2,256,256]{2,1,0:T(8,128)(2,1)S(1)}, u32[]{:S(2)}, u32[]{:S(2)}) collective-permute-start(bf16[2,256,256]{2,1,0:T(8,128)(2,1)} %bitcast.12), channel_id=1, source_target_pairs={{0,2},{1,5},{2,0},{3,7},{4,6},{5,1},{6,4},{7,3},{8,10},{9,13},{10,... | collective-permute-start | bytes 786440 | tf_op jit(solution)/shard_map/ppermute | solution.py:177
  3.8 1.0 %shard_map.59 = (bf16[2,256,256]{2,1,0:T(8,128)(2,1)S(1)}, bf16[2,256,256]{2,1,0:T(8,128)(2,1)S(1)}, bf16[2,256,256]{2,1,0:T(8,128)(2,1)S(1)}) custom-call(s32[1]{0:T(128)} %bitcast.slab_ref, bf16[2,256,256]{2,1,0:T(8,128)(2,1)} %bitcast.13, bf16[2,256,256]{2,1,0:T(8,128)(2,1)} %bitcast.10), custom_call_target="tpu_custom_call" | custom-call | flops 268435456 | bytes 1572864 | tf_op jit(solution)/shard_map/pallas_call | solution.py:203
  4.8 0.0 collective-permute-done.before_ref
  4.9 1.6 %collective-permute-start.2 = (bf16[2,256,256]{2,1,0:T(8,128)(2,1)S(1)}, bf16[2,256,256]{2,1,0:T(8,128)(2,1)S(1)}, u32[]{:S(2)}, u32[]{:S(2)}) collective-permute-start(bf16[2,256,256]{2,1,0:T(8,128)(2,1)S(1)} %shard_map.60.green_ref.own_ref.two_ref), channel_id=1, source_target_pairs={{0,4},{1,31},{2,6},{3,5},{4,0},{5,3},{6,2},{7,9},{8,12},{9,7},{10,... | collective-permute-start | bytes 786440 | tf_op jit(solution)/shard_map/ppermute | solution.py:177
  6.4 1.9 %collective-permute-done.1.one_ref = bf16[2,256,256]{2,1,0:T(8,128)(2,1)S(1)} collective-permute-done((bf16[2,256,256]{2,1,0:T(8,128)(2,1)}, bf16[2,256,256]{2,1,0:T(8,128)(2,1)S(1)}, u32[]{:S(2)}, u32[]{:S(2)}) %collective-permute-start.1) | collective-permute-done | bytes 262176 | tf_op jit(solution)/shard_map/ppermute | solution.py:177
  8.4 2.1 %collective-permute-start.3 = (bf16[2,256,256]{2,1,0:T(8,128)(2,1)S(1)}, bf16[2,256,256]{2,1,0:T(8,128)(2,1)S(1)}, u32[]{:S(2)}, u32[]{:S(2)}) collective-permute-start(bf16[2,256,256]{2,1,0:T(8,128)(2,1)S(1)} %shard_map.63), channel_id=1, source_target_pairs={{0,4},{1,3},{2,30},{3,1},{4,8},{5,7},{6,2},{7,5},{8,12},{9,11},{10... | collective-permute-start | bytes 786440 | tf_op jit(solution)/shard_map/ppermute | solution.py:177
  10.5 0.0 copy-done.1
  10.5 0.0 copy-done
  10.5 1.3 %shard_map.61 = (f32[3,2,256,256]{3,2,1,0:T(8,128)S(1)}, bf16[2,256,256]{2,1,0:T(8,128)(2,1)}) custom-call(s32[8]{0:T(128)S(1)} %copy-done.1, s32[1]{0:T(128)S(6)} %select_n.12.toward_ref, bf16[8,2,256,256]{3,2,1,0:T(8,128)(2,1)S(1)} %bitcast.8, bf16[2,256,256]{2,1,0:T(8,128)(2,1)S(1)} %shard_map.60.green_ref.own_ref.two_ref), custom_call_target="tpu_custom_call" | custom-call | bytes 3670016 | tf_op jit(solution)/shard_map/pallas_call | solution.py:227
  11.7 1.3 %collective-permute-done.2.two_ref = bf16[2,256,256]{2,1,0:T(8,128)(2,1)S(1)} collective-permute-done((bf16[2,256,256]{2,1,0:T(8,128)(2,1)S(1)}, bf16[2,256,256]{2,1,0:T(8,128)(2,1)S(1)}, u32[]{:S(2)}, u32[]{:S(2)}) %collective-permute-start.2) | collective-permute-done | bytes 262176 | tf_op jit(solution)/shard_map/ppermute | solution.py:177
  13.0 0.2 %shard_map.62.sum_ref = f32[2,256,256]{2,1,0:T(8,128)S(1)} custom-call(s32[1]{0:T(128)} %bitcast.slab_ref, bf16[2,256,256]{2,1,0:T(8,128)(2,1)S(1)} %shard_map.60.green_ref.own_ref.two_ref, bf16[2,256,256]{2,1,0:T(8,128)(2,1)S(1)} %collective-permute-done.1.one_ref, bf16[2,256,256]{2,1,0:T(8,128)(2,1)S(1)} %collective-permute-done.2.two_ref, ...), custom_call_target="tpu_custom_call" | custom-call | bytes 2621440 | tf_op jit(solution)/shard_map/pallas_call | solution.py:236
  13.2 4.7 %collective-permute-done.3.far_ref = bf16[2,256,256]{2,1,0:T(8,128)(2,1)S(1)} collective-permute-done((bf16[2,256,256]{2,1,0:T(8,128)(2,1)S(1)}, bf16[2,256,256]{2,1,0:T(8,128)(2,1)S(1)}, u32[]{:S(2)}, u32[]{:S(2)}) %collective-permute-start.3) | collective-permute-done | bytes 262176 | tf_op jit(solution)/shard_map/ppermute | solution.py:177
  18.0 0.9 %shard_map.64 = f32[2,256,256]{2,1,0:T(8,128)} custom-call(f32[2,256,256]{2,1,0:T(8,128)S(1)} %shard_map.62.sum_ref, bf16[2,256,256]{2,1,0:T(8,128)(2,1)S(1)} %collective-permute-done.3.far_ref, f32[3,2,256,256]{3,2,1,0:T(8,128)S(1)} %get-tuple-element.11.total_ref), custom_call_target="tpu_custom_call" | custom-call | bytes 2621440 | tf_op jit(solution)/shard_map/pallas_call | solution.py:244
  (2 shorter events, 0.1 us)
Async XLA Ops:
  0.6 9.8 %copy-start.1 = (s32[8]{0:T(128)S(1)}, s32[8]{0:T(128)}, u32[]{:S(2)}) copy-start(s32[8]{0:T(128)} %offset_ref.1) | copy-start | bytes 100
  0.6 9.8 %copy-start = (bf16[8,1,2,256,256]{4,3,2,1,0:T(8,128)(2,1)S(1)}, bf16[8,1,2,256,256]{4,3,2,1,0:T(8,128)(2,1)}, u32[]{:S(2)}) copy-start(bf16[8,1,2,256,256]{4,3,2,1,0:T(8,128)(2,1)} %param.6) | copy-start | bytes 6291460
  0.7 4.2 %collective-permute-start = (bf16[2,256,256]{2,1,0:T(8,128)(2,1)}, bf16[2,256,256]{2,1,0:T(8,128)(2,1)S(1)}, u32[]{:S(2)}, u32[]{:S(2)}) collective-permute-start(bf16[2,256,256]{2,1,0:T(8,128)(2,1)} %bitcast.11), channel_id=1, source_target_pairs={{0,1},{1,0},{2,3},{3,2},{4,5},{5,4},{6,7},{7,6},{8,9},{9,8},{10,11... | collective-permute-start | bytes 786440 | tf_op jit(solution)/shard_map/ppermute | solution.py:189
  1.2 7.1 %collective-permute-start.1 = (bf16[2,256,256]{2,1,0:T(8,128)(2,1)}, bf16[2,256,256]{2,1,0:T(8,128)(2,1)S(1)}, u32[]{:S(2)}, u32[]{:S(2)}) collective-permute-start(bf16[2,256,256]{2,1,0:T(8,128)(2,1)} %bitcast.12), channel_id=1, source_target_pairs={{0,2},{1,5},{2,0},{3,7},{4,6},{5,1},{6,4},{7,3},{8,10},{9,13},{10,... | collective-permute-start | bytes 786440 | tf_op jit(solution)/shard_map/ppermute | solution.py:177
  4.9 8.1 %collective-permute-start.2 = (bf16[2,256,256]{2,1,0:T(8,128)(2,1)S(1)}, bf16[2,256,256]{2,1,0:T(8,128)(2,1)S(1)}, u32[]{:S(2)}, u32[]{:S(2)}) collective-permute-start(bf16[2,256,256]{2,1,0:T(8,128)(2,1)S(1)} %shard_map.60.green_ref.own_ref.two_ref), channel_id=1, source_target_pairs={{0,4},{1,31},{2,6},{3,5},{4,0},{5,3},{6,2},{7,9},{8,12},{9,7},{10,... | collective-permute-start | bytes 786440 | tf_op jit(solution)/shard_map/ppermute | solution.py:177
  8.4 9.6 %collective-permute-start.3 = (bf16[2,256,256]{2,1,0:T(8,128)(2,1)S(1)}, bf16[2,256,256]{2,1,0:T(8,128)(2,1)S(1)}, u32[]{:S(2)}, u32[]{:S(2)}) collective-permute-start(bf16[2,256,256]{2,1,0:T(8,128)(2,1)S(1)} %shard_map.63), channel_id=1, source_target_pairs={{0,4},{1,3},{2,30},{3,1},{4,8},{5,7},{6,2},{7,5},{8,12},{9,11},{10... | collective-permute-start | bytes 786440 | tf_op jit(solution)/shard_map/ppermute | solution.py:177

commit v3 on v2

--- a/solution.py
+++ b/solution.py
@@ -25,19 +25,11 @@
     return dot(a[0], b[0]) - dot(a[1], b[1]), dot(a[0], b[1]) + dot(a[1], b[0])
 
 
-def load_kernel(slab_ref, free_hbm, coupling_hbm, free_ref, left_ref, right_ref, coupling_ref, sems):
-    copies = [
-        pltpu.make_async_copy(free_hbm, free_ref, sems.at[0]),
-        pltpu.make_async_copy(coupling_hbm, coupling_ref, sems.at[1]),
-    ]
-    for copy in copies:
-        copy.start()
-    for copy in copies:
-        copy.wait()
-    write_maps(slab_ref, free_ref, coupling_ref, left_ref, right_ref)
-
-
-def write_maps(slab_ref, free_ref, coupling_ref, left_ref, right_ref):
+def mark_kernel(slab_ref, out_ref):
+    out_ref[0] = slab_ref[0]
+
+
+def maps_kernel(slab_ref, free_ref, coupling_ref, left_ref, right_ref):
     @pl.when(slab_ref[0] > 0)
     def _():
         free = free_ref[0], free_ref[1]
@@ -86,16 +78,6 @@
         real = one if real is None else real + one
         imag = two if imag is None else imag + two
     return real, imag
-
-
-def pick_kernel(slab_ref, one_ref, two_ref, out_ref):
-    @pl.when(slab_ref[0] == 0)
-    def _():
-        out_ref[...] = one_ref[...]
-
-    @pl.when(slab_ref[0] != 0)
-    def _():
-        out_ref[...] = two_ref[...]
 
 
 def partial_kernel(slab_ref, own_ref, one_ref, two_ref, total_ref, sum_ref):
@@ -137,10 +119,6 @@
 PARAMS = pltpu.CompilerParams(vmem_limit_bytes=16 * 2**20)
 
 
-def in_hbm(array):
-    return pltpu.with_memory_space_constraint(array, pltpu.HBM)
-
-
 def in_vmem(shape, dtype):
     return pltpu.VMEM(shape, dtype)
 
@@ -159,12 +137,10 @@
     if count % 2 == 0:
         near = [e ^ 1 for e in range(count)]
         far = [(e + 1 if e % 2 else e - 1) % count for e in range(count)]
-        onward = [(e - 2 if e % 2 else e + 2) % count for e in range(count)]
         toward_near = 2 * (lax.axis_index("energy") % 2) - 1
     else:
         near = after
         far = [(e - 1) % count for e in range(count)]
-        onward = [(e - 2) % count for e in range(count)]
         toward_near = 1
     idle = [e ^ 2 for e in range(count)] if count % 4 == 0 else after
     toward = jnp.where(slab == 0, toward_near, -toward_near).astype(jnp.int32)
@@ -198,32 +174,36 @@
             compiler_params=PARAMS,
         )(slab, before, now, left, right)
 
+    def mark(value, flops):
+        return pl.pallas_call(
+            mark_kernel,
+            out_shape=pltpu.SMEM((1,), jnp.int32),
+            in_specs=[SMEM],
+            out_specs=SMEM,
+            cost_estimate=pl.CostEstimate(flops=flops, bytes_accessed=1024, transcendentals=0),
+            compiler_params=PARAMS,
+        )(value)
+
+    slab = mark(slab, 2**29)
     before = swap(free)
     first = exchange(free, near, idle)
-    own, left, right = pl.pallas_call(
-        load_kernel,
-        out_shape=(small,) * 3,
-        in_specs=[SMEM, HBM, HBM],
-        out_specs=[VMEM] * 3,
-        scratch_shapes=[small, pltpu.SemaphoreType.DMA((2,))],
-        cost_estimate=cost(2 * product, 6),
-        compiler_params=PARAMS,
-    )(slab, in_hbm(free), in_hbm(coupled))
+    slab = mark(slab, 2**31)
+    left, right = pl.pallas_call(
+        maps_kernel,
+        out_shape=(small,) * 2,
+        in_specs=[SMEM, VMEM, VMEM],
+        out_specs=[VMEM] * 2,
+        cost_estimate=cost(2 * product, 4),
+        compiler_params=PARAMS,
+    )(slab, free, coupled)
+    own = free
     green = own
     for step in range(1, segments):
         green = advance(step, before, green, left, right)
         if step < segments - 1:
             before = swap(green)
     second = exchange(green, idle, far)
-    payload = pl.pallas_call(
-        pick_kernel,
-        out_shape=small,
-        in_specs=[SMEM, VMEM, VMEM],
-        out_specs=VMEM,
-        cost_estimate=cost(0, 3),
-        compiler_params=PARAMS,
-    )(slab, first, green)
-    third = exchange(payload, onward, near)
+    third = exchange(green, far, near)
     total, green_out = pl.pallas_call(
         weights_kernel,
         out_shape=(in_vmem((3,) + block, jnp.float32), jax.ShapeDtypeStruct(block, jnp.bfloat16)),

time: 19 us -> 18.9 us (level)
  starting transfers between devices: 6.8 us -> 8.31 us
  waiting for transfers between devices: 7.87 us -> 6.44 us
  Pallas kernels: 3.47 us -> 2.35 us
  local copies, waits for them, and re-layouts: 0.01 us -> 1.02 us
    ppermute x3, starting transfers between devices: 6.24 us -> 7.75 us  [exchange(): return lax.ppermute(part, ('energy', 'slab'), pairs)]
    ppermute x3, waiting for transfers between devices: 7.87 us -> 6.44 us  [exchange(): return lax.ppermute(part, ('energy', 'slab'), pairs)]
    pallas_call x2 -> x3, Pallas kernels: 1.07 us -> 0.01 us  [the longest x2 0.01 us: mark(): pl.pallas_call(mark_kernel, out_shape=pltpu.SMEM((1,), jnp.int32), in_spe...]
    unnamed x4 -> x8, local copies, waits for them, and re-layouts: 0.01 us -> 1.02 us
  transfers between devices with their start and end apart: 4 -> 4, of which waited for: 3 -> 2; matrix products, arithmetic and copies ran while one was open for 0% -> 0% of each run, Pallas kernels for 14% -> 8%
where the time goes in v3:
time: 18.9 us; the launch traced here: 18.8 us
  starting transfers between devices  8.31 us (44%)
  waiting for transfers between devices  6.44 us (34%)
  Pallas kernels  2.35 us (12%)
  local copies, waits for them, and re-layouts  1.02 us (5%)
  between operations  0.68 us (4%)
    ppermute x3, starting transfers between devices, exchange(): return lax.ppermute(part, ('energy', 'slab'), pairs)  7.75 us
    ppermute x3, waiting for transfers between devices, exchange(): return lax.ppermute(part, ('energy', 'slab'), pairs)  6.44 us
    pallas_call x1, Pallas kernels, shards(): pl.pallas_call(weights_kernel, out_shape=(in_vmem((3,) + block, jnp.float...  1.25 us
    unnamed x8, local copies, waits for them, and re-layouts  1.02 us
    pallas_call x1, Pallas kernels, shards(): pl.pallas_call(far_kernel, out_shape=jax.ShapeDtypeStruct(block, jnp.floa...  0.88 us
    ppermute x1, starting transfers between devices, swap(): return lax.ppermute(part, 'slab', ring)  0.56 us
  transfers between devices with their start and end apart: 4, of which 2 were waited for; matrix products, arithmetic and copies ran while one was open for 0% of the time, Pallas kernels for 8%

profile of v3, /device:TPU:0, one launch (start us, length us, event | category | flops | bytes accessed | tf_op | source)
XLA Modules:
  0.0 18.8 jit_solution(5789963090256176286)
XLA Ops:
  0.6 0.6 %collective-permute-start = (bf16[2,256,256]{2,1,0:T(8,128)(2,1)}, bf16[2,256,256]{2,1,0:T(8,128)(2,1)S(1)}, u32[]{:S(2)}, u32[]{:S(2)}) collective-permute-start(bf16[2,256,256]{2,1,0:T(8,128)(2,1)} %bitcast.9), channel_id=1, source_target_pairs={{0,1},{1,0},{2,3},{3,2},{4,5},{5,4},{6,7},{7,6},{8,9},{9,8},{10,11... | collective-permute-start | bytes 786440 | tf_op jit(solution)/shard_map/ppermute | solution.py:165
  1.2 2.6 %collective-permute-start.1 = (bf16[2,256,256]{2,1,0:T(8,128)(2,1)}, bf16[2,256,256]{2,1,0:T(8,128)(2,1)S(1)}, u32[]{:S(2)}, u32[]{:S(2)}) collective-permute-start(bf16[2,256,256]{2,1,0:T(8,128)(2,1)} %bitcast.10), channel_id=1, source_target_pairs={{0,2},{1,5},{2,0},{3,7},{4,6},{5,1},{6,4},{7,3},{8,10},{9,13},{10,... | collective-permute-start | bytes 786440 | tf_op jit(solution)/shard_map/ppermute | solution.py:153
  3.7 0.0 copy-start.1
  3.7 0.0 copy-start.3
  3.7 0.0 copy-start
  3.8 0.0 copy-start.2
  3.8 1.0 %copy-done.1 = bf16[1,1,2,256,256]{4,3,2,1,0:T(8,128)(2,1)S(1)} copy-done((bf16[1,1,2,256,256]{4,3,2,1,0:T(8,128)(2,1)S(1)}, bf16[1,1,2,256,256]{4,3,2,1,0:T(8,128)(2,1)}, u32[]{:S(2)}) %copy-start.1) | copy-done | bytes 262168
  4.7 0.0 copy-done.3
  4.8 0.0 collective-permute-done.before_ref
  4.8 1.6 %collective-permute-start.2 = (bf16[2,256,256]{2,1,0:T(8,128)(2,1)S(1)}, bf16[2,256,256]{2,1,0:T(8,128)(2,1)S(1)}, u32[]{:S(2)}, u32[]{:S(2)}) collective-permute-start(bf16[2,256,256]{2,1,0:T(8,128)(2,1)S(1)} %shard_map.62.green_ref.own_ref), channel_id=1, source_target_pairs={{0,4},{1,31},{2,6},{3,5},{4,0},{5,3},{6,2},{7,9},{8,12},{9,7},{10,... | collective-permute-start | bytes 786440 | tf_op jit(solution)/shard_map/ppermute | solution.py:153
  6.4 3.6 %collective-permute-start.3 = (bf16[2,256,256]{2,1,0:T(8,128)(2,1)S(1)}, bf16[2,256,256]{2,1,0:T(8,128)(2,1)S(1)}, u32[]{:S(2)}, u32[]{:S(2)}) collective-permute-start(bf16[2,256,256]{2,1,0:T(8,128)(2,1)S(1)} %shard_map.62.green_ref.own_ref), channel_id=1, source_target_pairs={{0,30},{1,3},{2,4},{3,1},{4,2},{5,7},{6,8},{7,5},{8,6},{9,11},{10,... | collective-permute-start | bytes 786440 | tf_op jit(solution)/shard_map/ppermute | solution.py:153
  10.0 0.0 copy-done
  10.0 0.0 copy-done.2
  10.0 1.3 %shard_map.63 = (f32[3,2,256,256]{3,2,1,0:T(8,128)S(1)}, bf16[2,256,256]{2,1,0:T(8,128)(2,1)}) custom-call(s32[8]{0:T(128)S(1)} %copy-done.2, s32[1]{0:T(128)S(6)} %select_n.12.toward_ref, bf16[8,2,256,256]{3,2,1,0:T(8,128)(2,1)S(1)} %bitcast.8, bf16[2,256,256]{2,1,0:T(8,128)(2,1)S(1)} %shard_map.62.green_ref.own_ref), custom_call_target="tpu_custom_call" | custom-call | bytes 3670016 | tf_op jit(solution)/shard_map/pallas_call | solution.py:207
  11.3 0.0 collective-permute-done.1.one_ref
  11.3 4.5 %collective-permute-done.2.two_ref = bf16[2,256,256]{2,1,0:T(8,128)(2,1)S(1)} collective-permute-done((bf16[2,256,256]{2,1,0:T(8,128)(2,1)S(1)}, bf16[2,256,256]{2,1,0:T(8,128)(2,1)S(1)}, u32[]{:S(2)}, u32[]{:S(2)}) %collective-permute-start.2) | collective-permute-done | bytes 262176 | tf_op jit(solution)/shard_map/ppermute | solution.py:153
  15.8 0.2 %shard_map.64.sum_ref = f32[2,256,256]{2,1,0:T(8,128)S(1)} custom-call(s32[1]{0:T(128)S(4)} %shard_map.60.slab_ref, bf16[2,256,256]{2,1,0:T(8,128)(2,1)S(1)} %shard_map.62.green_ref.own_ref, bf16[2,256,256]{2,1,0:T(8,128)(2,1)S(1)} %collective-permute-done.1.one_ref, bf16[2,256,256]{2,1,0:T(8,128)(2,1)S(1)} %collective-permute-done.2.two_ref, ...), custom_call_target="tpu_custom_call" | custom-call | bytes 2621440 | tf_op jit(solution)/shard_map/pallas_call | solution.py:216
  16.0 1.9 %collective-permute-done.3.far_ref = bf16[2,256,256]{2,1,0:T(8,128)(2,1)S(1)} collective-permute-done((bf16[2,256,256]{2,1,0:T(8,128)(2,1)S(1)}, bf16[2,256,256]{2,1,0:T(8,128)(2,1)S(1)}, u32[]{:S(2)}, u32[]{:S(2)}) %collective-permute-start.3) | collective-permute-done | bytes 262176 | tf_op jit(solution)/shard_map/ppermute | solution.py:153
  17.9 0.9 %shard_map.65 = f32[2,256,256]{2,1,0:T(8,128)} custom-call(f32[2,256,256]{2,1,0:T(8,128)S(1)} %shard_map.64.sum_ref, bf16[2,256,256]{2,1,0:T(8,128)(2,1)S(1)} %collective-permute-done.3.far_ref, f32[3,2,256,256]{3,2,1,0:T(8,128)S(1)} %get-tuple-element.9.total_ref), custom_call_target="tpu_custom_call" | custom-call | bytes 2621440 | tf_op jit(solution)/shard_map/pallas_call | solution.py:224
  (4 shorter events, 0.0 us)
Async XLA Ops:
  0.6 4.1 %collective-permute-start = (bf16[2,256,256]{2,1,0:T(8,128)(2,1)}, bf16[2,256,256]{2,1,0:T(8,128)(2,1)S(1)}, u32[]{:S(2)}, u32[]{:S(2)}) collective-permute-start(bf16[2,256,256]{2,1,0:T(8,128)(2,1)} %bitcast.9), channel_id=1, source_target_pairs={{0,1},{1,0},{2,3},{3,2},{4,5},{5,4},{6,7},{7,6},{8,9},{9,8},{10,11... | collective-permute-start | bytes 786440 | tf_op jit(solution)/shard_map/ppermute | solution.py:165
  1.2 10.1 %collective-permute-start.1 = (bf16[2,256,256]{2,1,0:T(8,128)(2,1)}, bf16[2,256,256]{2,1,0:T(8,128)(2,1)S(1)}, u32[]{:S(2)}, u32[]{:S(2)}) collective-permute-start(bf16[2,256,256]{2,1,0:T(8,128)(2,1)} %bitcast.10), channel_id=1, source_target_pairs={{0,2},{1,5},{2,0},{3,7},{4,6},{5,1},{6,4},{7,3},{8,10},{9,13},{10,... | collective-permute-start | bytes 786440 | tf_op jit(solution)/shard_map/ppermute | solution.py:153
  3.7 1.0 %copy-start.1 = (bf16[1,1,2,256,256]{4,3,2,1,0:T(8,128)(2,1)S(1)}, bf16[1,1,2,256,256]{4,3,2,1,0:T(8,128)(2,1)}, u32[]{:S(2)}) copy-start(bf16[1,1,2,256,256]{4,3,2,1,0:T(8,128)(2,1)} %param.4) | copy-start | bytes 786436
  3.7 1.0 %copy-start.3 = (bf16[1,2,256,256]{3,2,1,0:T(8,128)(2,1)S(1)}, bf16[1,2,256,256]{3,2,1,0:T(8,128)(2,1)}, u32[]{:S(2)}) copy-start(bf16[1,2,256,256]{3,2,1,0:T(8,128)(2,1)} %param.5) | copy-start | bytes 786436
  3.7 6.2 %copy-start = (bf16[8,1,2,256,256]{4,3,2,1,0:T(8,128)(2,1)S(1)}, bf16[8,1,2,256,256]{4,3,2,1,0:T(8,128)(2,1)}, u32[]{:S(2)}) copy-start(bf16[8,1,2,256,256]{4,3,2,1,0:T(8,128)(2,1)} %param.6) | copy-start | bytes 6291460
  3.8 6.2 %copy-start.2 = (s32[8]{0:T(128)S(1)}, s32[8]{0:T(128)}, u32[]{:S(2)}) copy-start(s32[8]{0:T(128)} %offset_ref.1) | copy-start | bytes 100
  4.8 11.0 %collective-permute-start.2 = (bf16[2,256,256]{2,1,0:T(8,128)(2,1)S(1)}, bf16[2,256,256]{2,1,0:T(8,128)(2,1)S(1)}, u32[]{:S(2)}, u32[]{:S(2)}) collective-permute-start(bf16[2,256,256]{2,1,0:T(8,128)(2,1)S(1)} %shard_map.62.green_ref.own_ref), channel_id=1, source_target_pairs={{0,4},{1,31},{2,6},{3,5},{4,0},{5,3},{6,2},{7,9},{8,12},{9,7},{10,... | collective-permute-start | bytes 786440 | tf_op jit(solution)/shard_map/ppermute | solution.py:153
  6.4 11.5 %collective-permute-start.3 = (bf16[2,256,256]{2,1,0:T(8,128)(2,1)S(1)}, bf16[2,256,256]{2,1,0:T(8,128)(2,1)S(1)}, u32[]{:S(2)}, u32[]{:S(2)}) collective-permute-start(bf16[2,256,256]{2,1,0:T(8,128)(2,1)S(1)} %shard_map.62.green_ref.own_ref), channel_id=1, source_target_pairs={{0,30},{1,3},{2,4},{3,1},{4,2},{5,7},{6,8},{7,5},{8,6},{9,11},{10,... | collective-permute-start | bytes 786440 | tf_op jit(solution)/shard_map/ppermute | solution.py:153
